TPU v7x, 32 devices: a whole 2x2x4 slice. The times are simulated.
32 devices in a mesh: head: 8 (over y, x, core), tail: 4 (over z).
Axes of the slice: x: 2, y: 2, z: 4, core: 2. Of those that a mesh axis runs over, the one named last changes fastest.
Arguments:
- head_emb: float32 [8, 512, 256], P('head'), may hold values from -1.5 to 1.5
- tail_emb: float32 [4, 2048, 256], P('tail'), may hold values from -1.5 to 1.5
- relations: float32 [4096, 256], P(('head', 'tail')), may hold values from -0.375 to 0.375
- head_index: int32 [8, 4, 2, 1, 512], P('head', 'tail'), may hold values from 0 to 511
- tail_index: int32 [8, 4, 2, 1, 512], P('head', 'tail'), may hold values from 0 to 2047
- rel_index: int32 [8, 4, 2, 1, 512], P('head', 'tail'), may hold values from 0 to 15
- neg_index: int32 [8, 4, 2, 1, 512], P('head', 'tail'), may hold values from 0 to 2047
Outputs:
- head_grad: float32 [8, 512, 256], P('head', 'tail')
- tail_grad: float32 [4, 2048, 256], P('tail', 'head')
- rel_grad: float32 [4096, 256], P(('head', 'tail'))
All inputs are finite; a program needn't handle non-finite values.
Results may differ from a plain program's by a relative error of at most 0.00028.
Values sent between devices are 32-bit elements; how exact they have to be, the bound alone decides.
A program may use at most 128 MiB of HBM per device.

v0:
```python
import jax
import jax.numpy as jnp
from jax import lax
from jax.sharding import PartitionSpec as P


def from_behind(array, axis, by):
    devices = lax.axis_size(axis)
    return lax.ppermute(array, axis, [(i, (i + by) % devices) for i in range(devices)])


def per_device(head_emb, tail_emb, relations, head_index, tail_index, rel_index, neg_index):
    highest = lax.Precision.HIGHEST
    width = relations.shape[1]
    all_rel = lax.all_gather(relations, ("head", "tail"), axis=0, tiled=True)
    count_rel = all_rel.shape[0] // width
    rel_mats = all_rel.reshape(count_rel, width, width)
    rel_trans = jnp.transpose(rel_mats, (0, 2, 1))
    heads = head_emb[0]
    current = tail_emb[0]
    steps = head_index.shape[2]
    batch = head_index.shape[4]
    head_acc = jnp.zeros(heads.shape, jnp.float32)
    moving = jnp.zeros(current.shape, jnp.float32)
    spread_rows = []
    factors = []
    rel_ids = jnp.arange(count_rel, dtype=jnp.int32)
    for step in range(steps):
        if step > 0:
            current, moving = from_behind((current, moving), "tail", 1)
        local = jnp.zeros(current.shape, jnp.float32)
        order = jnp.argsort(rel_index[0, 0, step, 0], stable=True)
        rows_h = head_index[0, 0, step, 0][order]
        rows_t = tail_index[0, 0, step, 0][order]
        rows_r = rel_index[0, 0, step, 0][order]
        rows_n = neg_index[0, 0, step, 0]
        head_vec = jnp.take(heads, rows_h, axis=0)
        onehot = (rows_r[:, None] == rel_ids[None, :]).astype(jnp.float32)
        group_sizes = jnp.sum((rows_r[:, None] == rel_ids[None, :]).astype(jnp.int32), axis=0)
        query = lax.ragged_dot(
            head_vec, rel_mats, group_sizes, precision=highest, preferred_element_type=jnp.float32
        )
        tail_vec = jnp.take(current, rows_t, axis=0)
        negatives = jnp.take(current, rows_n, axis=0)
        positive = jnp.sum(query * tail_vec, axis=1)
        negative = jnp.einsum("be,ne->bn", query, negatives, precision=highest)
        coef = -jax.nn.sigmoid(-positive)
        weights = jax.nn.sigmoid(negative) / negatives.shape[0]
        factor = coef[:, None] * tail_vec + jnp.dot(weights, negatives, precision=highest)
        through = lax.ragged_dot(
            factor, rel_trans, group_sizes, precision=highest, preferred_element_type=jnp.float32
        )
        head_acc = head_acc.at[rows_h].add(through)
        local = local.at[rows_t].add(coef[:, None] * query)
        local = local.at[rows_n].add(jnp.einsum("bn,be->ne", weights, query, precision=highest))
        spread = (onehot[:, :, None] * head_vec[:, None, :]).reshape(batch, count_rel * width)
        spread_rows.append(spread)
        factors.append(factor)
        moving = moving + local
    back_home = from_behind(moving, "tail", -(steps - 1))
    tail_share = lax.psum_scatter(back_home, "head", scatter_dimension=0, tiled=True)
    head_share = lax.psum_scatter(head_acc, "tail", scatter_dimension=0, tiled=True)
    spread_all = jnp.concatenate(spread_rows, axis=0)
    factor_all = jnp.concatenate(factors, axis=0)
    full_term = jnp.einsum("bk,be->ke", spread_all, factor_all, precision=highest)
    middle = lax.psum_scatter(full_term, "head", scatter_dimension=0, tiled=True)
    rel_share = lax.psum_scatter(middle, "tail", scatter_dimension=0, tiled=True)
    return (head_share[None], tail_share[None], rel_share)


def solution(mesh):
    placed = (
        P("head", None, None),
        P("tail", None, None),
        P(("head", "tail"), None),
        P("head", "tail", None, None, None),
        P("head", "tail", None, None, None),
        P("head", "tail", None, None, None),
        P("head", "tail", None, None, None),
    )
    return jax.shard_map(
        per_device,
        mesh=mesh,
        in_specs=placed,
        out_specs=(P("head", "tail", None), P("tail", "head", None), P(("head", "tail"), None)),
        check_vma=False,
    )
```

profile of v0, /device:TPU:0, one launch (start us, length us, event | category | flops | bytes accessed | tf_op | source)
XLA Modules:
  0.0 391.4 jit_solution(16428537927477798335)
XLA Ops:
  11.8 3.8 sort.31
  26.1 3.8 sort.32
  40.2 5.0 %broadcast_multiply_fusion = f32[512,16,256]{2,1,0:T(8,128)} fusion(f32[512,256]{1,0:T(8,128)S(1)} %broadcast_select_fusion, f32[512,16]{1,0:T(8,128)S(1)} %copy.15), kind=kLoop, calls=%fused_computation.22 | loop fusion | flops 2097152 | bytes 8945664 | tf_op jit(solution)/shard_map/mul | solution.py:56
  58.1 14.7 %copy.17 = f32[64,8,16,256]{3,1,2,0:T(8,128)} copy(f32[64,8,16,256]{3,2,1,0:T(8,128)} %bitcast.55) | data formatting | bytes 16777216
  74.7 11.3 %copy.16 = f32[64,8,16,256]{3,1,2,0:T(8,128)} copy(f32[64,8,16,256]{3,2,1,0:T(8,128)S(1)} %bitcast.56) | data formatting | bytes 16777216
  86.1 3.8 gather_fusion.11
  93.1 13.5 %all-gather.2.cloned.1.call-done = f32[4096,256]{1,0:T(8,128)} async-done(((f32[128,256]{1,0:T(8,128)}), f32[4096,256]{1,0:T(8,128)}) %all-gather.2.cloned.1.call-update) | async-done | bytes 4194320 | tf_op jit(solution)/shard_map/all_gather | solution.py:15
  106.6 14.9 %ragged-dot-none.3 = f32[512,256]{1,0:T(8,128)} custom-call(s32[1]{0:T(128)} %get-tuple-element.17, s32[17]{0:T(128)} %get-tuple-element.18, s32[17]{0:T(128)} %get-tuple-element.19, s32[17]{0:T(128)} %get-tuple-element.20, s32[1]{0:T(128)} %get-tuple-element.17, f32[512,256]{1,0:T(8,128)} %copy-done.8, f32[16,256,256]{2,1,0:T(8,128)} %bitcast.50), custom_call_target="tpu_custom_call" | custom-call | flops 67108864 | bytes 5242944 | tf_op jit(solution)/shard_map/ragged_dot_general/ragged-dot-none
  122.8 15.0 %ragged-dot-none.1 = f32[512,256]{1,0:T(8,128)} custom-call(s32[1]{0:T(128)} %get-tuple-element.9, s32[17]{0:T(128)} %get-tuple-element.10, s32[17]{0:T(128)} %get-tuple-element.11, s32[17]{0:T(128)} %get-tuple-element.12, s32[1]{0:T(128)} %get-tuple-element.9, f32[512,256]{1,0:T(8,128)} %copy-done.7, f32[16,256,256]{2,1,0:T(8,128)} %bitcast.51), custom_call_target="tpu_custom_call" | custom-call | flops 67108864 | bytes 5242944 | tf_op jit(solution)/shard_map/ragged_dot_general/ragged-dot-none
  144.5 31.5 %fusion = f32[4096,256]{1,0:T(8,128)} fusion(f32[512,4096]{1,0:T(8,128)S(1)} %bitcast.62, f32[512,4096]{1,0:T(8,128)} %bitcast.63, f32[512,256]{1,0:T(8,128)S(1)} %multiply_add_fusion, f32[512,256]{1,0:T(8,128)S(1)} %convolution_add_fusion), kind=kOutput, calls=%fused_computation.18 | convolution fusion | flops 12889358336 | bytes 22020096 | tf_op jit(solution)/shard_map/bk,be->ke/dot_general | solution.py:65
  176.2 3.9 %scatter_custom_fusion.2 = f32[2048,256]{1,0:T(8,128)S(1)} fusion(s32[512]{0:T(512)S(1)} %bitcast.77, f32[]{:T(128)} %constant.22.clone.1, f32[512,256]{1,0:T(8,128)S(1)} %copy-done.5, f32[512]{0:T(512)S(1)} %divide_negate_fusion.1), kind=kCustom, calls=%fused_computation.38 | custom fusion | flops 262144 | bytes 2623492 | tf_op jit(solution)/shard_map/scatter-add | solution.py:54
  180.1 3.9 fusion.50
  184.0 4.6 %scatter_fusion.1 = f32[2048,256]{1,0:T(8,128)S(1)} fusion(f32[2048,256]{1,0:T(8,128)S(1)} %scatter_custom_fusion.2, s32[512]{0:T(512)S(1)} %bitcast.74, f32[512,256]{1,0:T(8,128)} %fusion.50), kind=kCustom, calls=%fused_computation.15 | custom fusion | flops 131072 | bytes 1574912 | tf_op jit(solution)/shard_map/scatter-add | solution.py:55
  193.3 45.0 %collective-permute-done.1 = f32[2048,256]{1,0:T(8,128)S(1)} collective-permute-done((f32[2048,256]{1,0:T(8,128)S(1)}, f32[2048,256]{1,0:T(8,128)S(1)}, u32[]{:S(2)}, u32[]{:S(2)}) %collective-permute-start.1) | collective-permute-done | bytes 2097184 | tf_op jit(solution)/shard_map/ppermute | solution.py:9
  239.7 6.1 %scatter_custom_fusion.4 = f32[2048,256]{1,0:T(8,128)} fusion(f32[2048,256]{1,0:T(8,128)} %copy-done.4, s32[512]{0:T(512)S(1)} %bitcast.76, f32[512,256]{1,0:T(8,128)S(1)} %copy-done.6, f32[512]{0:T(512)S(1)} %divide_negate_fusion), kind=kCustom, calls=%fused_computation.40 | custom fusion | flops 262144 | bytes 2623488 | tf_op jit(solution)/shard_map/scatter-add | solution.py:54
  245.8 6.2 %scatter_fusion.2 = f32[2048,256]{1,0:T(8,128)} fusion(f32[2048,256]{1,0:T(8,128)} %scatter_custom_fusion.4, s32[512]{0:T(512)S(1)} %bitcast.73, f32[512,256]{1,0:T(8,128)S(1)} %fusion.51), kind=kCustom, calls=%fused_computation.17 | custom fusion | flops 131072 | bytes 1574912 | tf_op jit(solution)/shard_map/scatter-add | solution.py:55
  252.3 5.4 %copy.13 = f32[16,256,256]{1,2,0:T(8,128)} copy(f32[16,256,256]{2,1,0:T(8,128)} %bitcast.52) | data formatting | bytes 8388608 | tf_op jit(solution)/shard_map/reshape | solution.py:17
  257.6 14.9 %ragged-dot-none.2 = f32[512,256]{1,0:T(8,128)} custom-call(s32[1]{0:T(128)} %get-tuple-element.17, s32[17]{0:T(128)} %get-tuple-element.18, s32[17]{0:T(128)} %get-tuple-element.19, s32[17]{0:T(128)} %get-tuple-element.20, s32[1]{0:T(128)} %get-tuple-element.17, f32[512,256]{1,0:T(8,128)} %copy-done.15, f32[16,256,256]{2,1,0:T(8,128)} %bitcast.53), custom_call_target="tpu_custom_call" | custom-call | flops 67108864 | bytes 5242944 | tf_op jit(solution)/shard_map/ragged_dot_general/ragged-dot-none
  272.5 3.9 %scatter_custom_fusion = f32[512,256]{1,0:T(8,128)S(1)} fusion(s32[512]{0:T(512)S(1)} %bitcast.75, f32[512,256]{1,0:T(8,128)} %ragged-dot-none.2, f32[]{:T(128)} %constant.22.clone.1), kind=kCustom, calls=%fused_computation.59 | custom fusion | flops 131072 | bytes 524800 | tf_op jit(solution)/shard_map/scatter-add | solution.py:53
  276.4 14.9 %ragged-dot-none = f32[512,256]{1,0:T(8,128)} custom-call(s32[1]{0:T(128)} %get-tuple-element.9, s32[17]{0:T(128)} %get-tuple-element.10, s32[17]{0:T(128)} %get-tuple-element.11, s32[17]{0:T(128)} %get-tuple-element.12, s32[1]{0:T(128)} %get-tuple-element.9, f32[512,256]{1,0:T(8,128)} %copy-done.14, f32[16,256,256]{2,1,0:T(8,128)} %bitcast.54), custom_call_target="tpu_custom_call" | custom-call | flops 67108864 | bytes 5242944 | tf_op jit(solution)/shard_map/ragged_dot_general/ragged-dot-none
  291.3 4.1 %scatter_fusion = f32[512,256]{1,0:T(8,128)S(1)} fusion(f32[512,256]{1,0:T(8,128)S(1)} %scatter_custom_fusion, s32[512]{0:T(512)S(1)} %bitcast.72, f32[512,256]{1,0:T(8,128)} %ragged-dot-none), kind=kCustom, calls=%fused_computation.13 | custom fusion | flops 131072 | bytes 1574912 | tf_op jit(solution)/shard_map/scatter-add | solution.py:53
  301.1 15.6 %reduce-scatter.5.cloned.1.call-done = f32[128,256]{1,0:T(8,128)} async-done(((f32[512,256]{1,0:T(8,128)}), f32[128,256]{1,0:T(8,128)}) %reduce-scatter.5.cloned.1.call-update) | async-done | bytes 131088 | tf_op jit(solution)/shard_map/reduce_scatter | solution.py:62
  316.7 43.2 %reduce-scatter.7.cloned.1.call-done = f32[256,256]{1,0:T(8,128)} async-done(((f32[2048,256]{1,0:T(8,128)}), f32[256,256]{1,0:T(8,128)}) %reduce-scatter.7.cloned.1.call-update) | async-done | bytes 262160 | tf_op jit(solution)/shard_map/reduce_scatter | solution.py:61
  359.9 24.5 %reduce-scatter.11.cloned.1.call-done = f32[128,256]{1,0:T(8,128)} async-done(((f32[512,256]{1,0:T(8,128)}), f32[128,256]{1,0:T(8,128)}) %reduce-scatter.11.cloned.1.call-update) | async-done | bytes 131088 | tf_op jit(solution)/shard_map/reduce_scatter | solution.py:67
  (125 shorter events, 63.1 us)
Async XLA Ops:
  7.2 29.9 %copy-start = (f32[1,512,256]{2,1,0:T(8,128)S(1)}, f32[1,512,256]{2,1,0:T(8,128)}, u32[]{:S(2)}) copy-start(f32[1,512,256]{2,1,0:T(8,128)} %param.11) | copy-start | bytes 1572868
  7.2 11.9 %copy-start.19 = (s32[1,1,2,1,512]{4,3,2,1,0:T(1,128)S(1)}, s32[1,1,2,1,512]{4,3,2,1,0:T(1,128)}, u32[]{:S(2)}) copy-start(s32[1,1,2,1,512]{4,3,2,1,0:T(1,128)} %param.15) | copy-start | bytes 12292
  7.2 99.4 %all-gather.2.cloned.1.call-start = ((), (), s32[]{:S(2)}) async-start(), calls=%async_computation.4 | async-start | bytes 4325376 | tf_op jit(solution)/shard_map/all_gather | solution.py:15
  7.9 292.6 %reduce-scatter.9.cloned.1.call-start = ((), (), s32[]{:S(2)}) async-start(), calls=%async_computation.7 | async-start | bytes 4718592 | tf_op jit(solution)/shard_map/reduce_scatter | solution.py:66
  8.0 78.2 %collective-permute-start = (f32[2048,256]{1,0:T(8,128)}, f32[2048,256]{1,0:T(8,128)}, u32[]{:S(2)}, u32[]{:S(2)}) collective-permute-start(f32[2048,256]{1,0:T(8,128)} %bitcast.57), channel_id=1, source_target_pairs={{0,1},{1,2},{2,3},{3,0},{4,5},{5,6},{6,7},{7,4},{8,9},{9,10},{10,1... | collective-permute-start | bytes 6291464 | tf_op jit(solution)/shard_map/ppermute | solution.py:9
  15.6 7.0 %copy-start.20 = (s32[1,1,2,1,512]{4,3,2,1,0:T(1,128)S(1)}, s32[1,1,2,1,512]{4,3,2,1,0:T(1,128)}, u32[]{:S(2)}) copy-start(s32[1,1,2,1,512]{4,3,2,1,0:T(1,128)} %param.14) | copy-start | bytes 12292
  37.1 2.9 copy-start.18
  40.2 5.0 %copy-start.7 = (f32[512,256]{1,0:T(8,128)}, f32[512,256]{1,0:T(8,128)S(1)}, u32[]{:S(2)}) copy-start(f32[512,256]{1,0:T(8,128)S(1)} %broadcast_select_fusion) | copy-start | bytes 1572868
  45.1 7.6 %copy-start.3 = (f32[1,2048,256]{2,1,0:T(8,128)S(1)}, f32[1,2048,256]{2,1,0:T(8,128)}, u32[]{:S(2)}) copy-start(f32[1,2048,256]{2,1,0:T(8,128)} %param.12) | copy-start | bytes 6291460
  56.6 64.9 %copy-start.9 = (f32[512,256]{1,0:T(8,128)}, f32[512,256]{1,0:T(8,128)S(1)}, u32[]{:S(2)}) copy-start(f32[512,256]{1,0:T(8,128)S(1)} %gather_fusion.7) | copy-start | bytes 1572868
  73.0 1.7 copy-start.8
  122.8 16.3 %copy-start.5 = (f32[512,256]{1,0:T(8,128)S(1)}, f32[512,256]{1,0:T(8,128)}, u32[]{:S(2)}) copy-start(f32[512,256]{1,0:T(8,128)} %ragged-dot-none.3) | copy-start | bytes 1572868
  122.8 16.3 %copy-start.16 = (f32[512,256]{1,0:T(8,128)S(1)}, f32[512,256]{1,0:T(8,128)}, u32[]{:S(2)}) copy-start(f32[512,256]{1,0:T(8,128)} %gather_fusion.8) | copy-start | bytes 1572868
  139.1 5.4 %slice-start = ((s8[8388608]{0:T(1024)(128)(4,1)}), s8[4194304]{0:T(1024)(128)(4,1)S(1)}, s32[]{:S(2)}) async-start(s8[8388608]{0:T(1024)(128)(4,1)} %bitcast.60), calls=%async_computation.9 | async-start | bytes 8388608
  141.6 2.9 copy-start.15
  142.1 2.4 slice-start.1
  143.4 32.7 %copy-start.11 = (f32[512,512]{1,0:T(8,128)}, f32[512,512]{1,0:T(8,128)S(1)}, u32[]{:S(2)}) copy-start(f32[512,512]{1,0:T(8,128)S(1)} %fusion.7) | copy-start | bytes 3145732
  144.5 31.6 %copy-start.14 = (f32[512,256]{1,0:T(8,128)}, f32[512,256]{1,0:T(8,128)S(1)}, u32[]{:S(2)}) copy-start(f32[512,256]{1,0:T(8,128)S(1)} %multiply_add_fusion) | copy-start | bytes 1572868
  176.1 140.6 %reduce-scatter.5.cloned.1.call-start = ((), (), s32[]{:S(2)}) async-start(), calls=%async_computation.5 | async-start | bytes 655360 | tf_op jit(solution)/shard_map/reduce_scatter | solution.py:62
  188.6 49.6 %collective-permute-start.1 = (f32[2048,256]{1,0:T(8,128)S(1)}, f32[2048,256]{1,0:T(8,128)S(1)}, u32[]{:S(2)}, u32[]{:S(2)}) collective-permute-start(f32[2048,256]{1,0:T(8,128)S(1)} %scatter_fusion.1), channel_id=1, source_target_pairs={{0,1},{1,2},{2,3},{3,0},{4,5},{5,6},{6,7},{7,4},{8,9},{9,10},{10,1... | collective-permute-start | bytes 6291464 | tf_op jit(solution)/shard_map/ppermute | solution.py:9
  252.0 47.1 %collective-permute-start.2 = (f32[2048,256]{1,0:T(8,128)}, f32[2048,256]{1,0:T(8,128)S(1)}, u32[]{:S(2)}, u32[]{:S(2)}) collective-permute-start(f32[2048,256]{1,0:T(8,128)} %scatter_fusion.2), channel_id=1, source_target_pairs={{0,3},{1,0},{2,1},{3,2},{4,7},{5,4},{6,5},{7,6},{8,11},{9,8},{10,9... | collective-permute-start | bytes 6291464 | tf_op jit(solution)/shard_map/ppermute | solution.py:9
  291.3 93.1 %copy-start.1 = (f32[1,512,256]{2,1,0:T(8,128)S(1)}, f32[1,512,256]{2,1,0:T(8,128)}, u32[]{:S(2)}) copy-start(f32[1,512,256]{2,1,0:T(8,128)} %param.11) | copy-start | bytes 1572868
  296.2 63.7 %reduce-scatter.7.cloned.1.call-start = ((), (), s32[]{:S(2)}) async-start(), calls=%async_computation.6 | async-start | bytes 2359296 | tf_op jit(solution)/shard_map/reduce_scatter | solution.py:61
  300.5 83.9 %reduce-scatter.11.cloned.1.call-start = ((), (), s32[]{:S(2)}) async-start(), calls=%async_computation.8 | async-start | bytes 655360 | tf_op jit(solution)/shard_map/reduce_scatter | solution.py:67
  (7 other events, 9.1 us)
Sparse Core Ops, SparseCore 0:
  11.0 95.5 all-gather.1
  176.2 49.9 reduce-scatter.8
  296.3 20.2 reduce-scatter.4
  320.4 39.4 reduce-scatter.6
  362.6 21.7 reduce-scatter.10
where the time goes:
time: 397 us; the launch traced here: 391 us
  waiting for transfers between devices  146 us (37%)
  local copies, waits for them, and re-layouts  71.4 us (18%)
  Pallas kernels  63.6 us (16%)
  other arithmetic  47.3 us (12%)
  matrix products  43.1 us (11%)
  between operations  14.9 us (4%)
  starting transfers between devices  5.16 us (1%)
    another operation x4, Pallas kernels  59.6 us
    ppermute x3, waiting for transfers between devices, from_behind(): lax.ppermute(array, axis, [(i, (i + by) % devices) for i in range(devices)])  47.9 us
    reduce_scatter x1, waiting for transfers between devices, per_device(): lax.psum_scatter(back_home, 'head', scatter_dimension=0, tiled=True)  43.2 us
    dot_general x1, matrix products, per_device(): jnp.einsum('bk,be->ke', spread_all, factor_all, precision=highest)  31.5 us
    unnamed x48, local copies, waits for them, and re-layouts  30.2 us
    reduce_scatter x1, waiting for transfers between devices, per_device(): lax.psum_scatter(middle, 'tail', scatter_dimension=0, tiled=True)  24.5 us
    reduce_scatter x1, waiting for transfers between devices, per_device(): lax.psum_scatter(head_acc, 'tail', scatter_dimension=0, tiled=True)  15.6 us
    all_gather x1, waiting for transfers between devices, per_device(): all_rel = lax.all_gather(relations, ('head', 'tail'), axis=0, tiled=True)  13.5 us
  transfers between devices with their start and end apart: 8, of which 6 were waited for; matrix products, arithmetic and copies ran while one was open for 30% of the time, Pallas kernels for 9%

commit v1 on v0

v1 whole, which is shorter than its diff:
```python
import functools
import jax
import jax.numpy as jnp
from jax import lax
from jax.experimental import pallas as pl
from jax.experimental.pallas import tpu as pltpu
from jax.sharding import PartitionSpec as P

F32 = jnp.float32
BF16 = jnp.bfloat16
VMEM_LIMIT = 60 * 1024 * 1024
NN = (((1,), (0,)), ((), ()))
NT = (((1,), (1,)), ((), ()))
TN = (((0,), (0,)), ((), ()))


def split(x):
    high = x.astype(BF16)
    return high, (x - high.astype(F32)).astype(BF16)


def dot(a, b, dims):
    return lax.dot_general(a, b, dims, preferred_element_type=F32)


def dot3(a, b, dims):
    return dot(a[0], b[0], dims) + (dot(a[0], b[1], dims) + dot(a[1], b[0], dims))


def log2(n):
    assert n & (n - 1) == 0
    return n.bit_length() - 1


class Bits:
    def __init__(self, sizes):
        self.names = [(axis, bit) for axis, size in sizes for bit in reversed(range(log2(size)))]

    def mine(self, i):
        axis, bit = self.names[i]
        return lax.rem(lax.axis_index(axis) // (1 << bit), 2)

    def partner(self, i):
        axis, bit = self.names[i]
        here = lax.axis_index(axis)
        return {axis: here + (1 << bit) * (1 - 2 * self.mine(i))}


def meet(partners):
    barrier = pltpu.get_barrier_semaphore()
    for device in partners:
        pl.semaphore_signal(barrier, inc=1, device_id=device, device_id_type=pl.DeviceIdType.MESH)
    pl.semaphore_wait(barrier, len(partners))


def gather_kernel(
    bits, orders, rel_ref, heads_ref, tails_ref, idx_ref,
    full_ref, hv_ref, tv_ref, nv_ref, heads_cat, tails_cat, send_sem, recv_sem,
):
    count = len(bits.names)
    parts = len(orders)
    rows = rel_ref.shape[0] // parts
    mine = [bits.mine(i) for i in range(count)]
    partner = [bits.partner(i) for i in range(count)]
    meet(partner)

    def start(part, stage):
        order = orders[part]
        done = set(order[:stage])
        where = tuple(slice(None) if i in done else mine[i] for i in range(count))
        where = where + (pl.ds(part * rows, rows),)
        source = rel_ref.at[pl.ds(part * rows, rows)] if stage == 0 else full_ref.at[where]
        copy = pltpu.make_async_remote_copy(
            src_ref=source,
            dst_ref=full_ref.at[where],
            send_sem=send_sem.at[part * count + stage],
            recv_sem=recv_sem.at[part * count + stage],
            device_id=partner[order[stage]],
            device_id_type=pl.DeviceIdType.MESH,
        )
        copy.start()
        return copy

    copies = [[start(part, 0)] for part in range(parts)]
    full_ref[tuple(mine)] = rel_ref[...]

    blocks, batch = idx_ref.shape[1], idx_ref.shape[2]
    width = heads_ref.shape[1]
    tile = 128

    def halves(source, cat):
        high, low = split(source[...])
        cat[:, :width] = high
        cat[:, width:] = low

    def take(which, b, cat, out):
        def body(t, carry):
            at = pl.ds(pl.multiple_of(t * tile, tile), tile)
            ids = idx_ref[which, b, at]
            hot = (ids == lax.broadcasted_iota(jnp.int32, (tile, cat.shape[0]), 1)).astype(BF16)
            both = dot(hot, cat[...], NN)
            out[b, at] = both[:, :width] + both[:, width:]
            return carry

        lax.fori_loop(0, batch // tile, body, 0)

    work = [lambda: (halves(heads_ref, heads_cat), halves(tails_ref, tails_cat))]
    work += [functools.partial(take, 0, b, heads_cat, hv_ref) for b in range(blocks)]
    work += [functools.partial(take, 1, b, tails_cat, tv_ref) for b in range(blocks)]
    work += [functools.partial(take, 2, b, tails_cat, nv_ref) for b in range(blocks)]
    per = -(-len(work) // count)
    for stage in range(count):
        for job in work[stage * per:(stage + 1) * per]:
            job()
        for part in range(parts):
            copies[part][stage].wait_recv()
            if stage + 1 < count:
                copies[part].append(start(part, stage + 1))
    for part in range(parts):
        for copy in copies[part]:
            copy.wait_send()


def compute_kernel(
    off_ref, rel_ref, hv_ref, tv_ref, nv_ref, idx_ref,
    head_ref, tail_ref, grad_ref,
    rel_hi, rel_lo, query, factor, through, spread,
):
    relations = off_ref.shape[1] - 1
    blocks, batch, width = hv_ref.shape
    negs = nv_ref.shape[1]
    window = 64
    row_id = lax.broadcasted_iota(jnp.int32, (window, 1), 0)

    def halve(r, carry):
        at = pl.ds(pl.multiple_of(r * width, width), width)
        rel_hi[at], rel_lo[at] = split(rel_ref[at])
        return carry

    lax.fori_loop(0, relations, halve, 0)
    query[...] = jnp.zeros_like(query)
    through[...] = jnp.zeros_like(through)

    def over_windows(step, after=None):
        def one(r, carry):
            low = [off_ref[b, r] for b in range(blocks)]
            high = [off_ref[b, r + 1] for b in range(blocks)]
            base = [low[b] // 8 * 8 for b in range(blocks)]
            trips = jnp.int32(0)
            for b in range(blocks):
                here = jnp.where(high[b] > low[b], (high[b] - base[b] + window - 1) // window, 0)
                trips = jnp.maximum(trips, here)
            at_r = pl.ds(pl.multiple_of(r * width, width), width)

            def inner(w, c):
                places, masks = [], []
                for b in range(blocks):
                    begin = base[b] + w * window
                    at = pl.multiple_of(jnp.minimum(begin, batch - window), 8)
                    first = jnp.maximum(low[b], begin)
                    last = jnp.minimum(high[b], begin + window)
                    ids = row_id + at
                    places.append(pl.ds(at, window))
                    masks.append(jnp.logical_and(ids >= first, ids < last))
                step(at_r, places, masks)
                return c

            lax.fori_loop(0, trips, inner, 0)
            return carry

        lax.fori_loop(0, relations, one, 0)

    def masked(ref, places, masks):
        return jnp.concatenate(
            [jnp.where(masks[b], ref[b, places[b]], 0.0) for b in range(blocks)], axis=0
        )

    def apply(source, out, dims):
        def step(at_r, places, masks):
            x = split(masked(source, places, masks))
            y = dot3(x, (rel_hi[at_r], rel_lo[at_r]), dims)
            for b in range(blocks):
                out[b, places[b]] += y[b * window:(b + 1) * window]
        return step

    over_windows(apply(hv_ref, query, NN))

    for b in range(blocks):
        q = query[b]
        tv = tv_ref[b]
        q2 = split(q)
        n2 = split(nv_ref[b])
        positive = jnp.sum(q * tv, axis=1, keepdims=True)
        coef = -jax.nn.sigmoid(-positive)
        weights = split(jax.nn.sigmoid(dot3(q2, n2, NT)) / negs)
        factor[b] = coef * tv + dot3(weights, n2, NN)
        rows = jnp.concatenate([coef * q, dot3(weights, q2, TN)], axis=0)
        high, low = split(rows)
        at = pl.ds(b * (batch + negs), batch + negs)
        spread[at, :width] = high
        spread[at, width:] = low

    grad_ref[...] = jnp.zeros_like(grad_ref)

    def outer(at_r, places, masks):
        x = split(masked(hv_ref, places, masks))
        f = split(jnp.concatenate([factor[b, places[b]] for b in range(blocks)], axis=0))
        grad_ref[at_r] += dot3(x, f, TN)

    over_windows(outer)
    over_windows(apply(factor, through, NT))

    tile = 256
    ids = idx_ref[1:2, :]

    def scatter(t, carry):
        at = pl.ds(pl.multiple_of(t * tile, tile), tile)
        hot = (ids == lax.broadcasted_iota(jnp.int32, (tile, ids.shape[1]), 0) + t * tile).astype(BF16)
        both = dot(hot, spread[...], NN)
        tail_ref[at] = both[:, :width] + both[:, width:]
        return carry

    lax.fori_loop(0, tail_ref.shape[0] // tile, scatter, 0)
    hids = idx_ref[0:1, :blocks * batch]
    hot = (hids == lax.broadcasted_iota(jnp.int32, (head_ref.shape[0], hids.shape[1]), 0)).astype(BF16)
    high, low = split(through[...].reshape(blocks * batch, width))
    head_ref[...] = dot(hot, high, NN) + dot(hot, low, NN)


def reduce_kernel(bits, plans, *refs):
    inputs = refs[:3]
    outs = refs[3:6]
    buffers = refs[6:-2]
    send_sem, recv_sem = refs[-2:]
    mine = [bits.mine(i) for i in range(len(bits.names))]
    partner = [bits.partner(i) for i in range(len(bits.names))]
    meet(partner)
    flows = []
    sem = 0
    buf = 0
    for array, order, part, parts in plans:
        rows = inputs[array].shape[-2] // parts
        flows.append(dict(
            array=array, order=order, rows=pl.ds(part * rows, rows), sem=sem,
            buffers=buffers[buf:buf + len(order)], left=sorted(order), copies=[],
        ))
        sem += len(order)
        buf += len(order)

    def cut(flow, stage, bit, value):
        place = flow["left"].index(bit)
        where = (slice(None),) * place + (value,)
        if stage == 0:
            where = where + (slice(None),) * (len(flow["left"]) - place - 1) + (flow["rows"],)
            return inputs[flow["array"]], where
        return flow["buffers"][stage - 1], where

    def start(flow, stage):
        bit = flow["order"][stage]
        ref, where = cut(flow, stage, bit, 1 - mine[bit])
        copy = pltpu.make_async_remote_copy(
            src_ref=ref.at[where],
            dst_ref=flow["buffers"][stage],
            send_sem=send_sem.at[flow["sem"] + stage],
            recv_sem=recv_sem.at[flow["sem"] + stage],
            device_id=partner[bit],
            device_id_type=pl.DeviceIdType.MESH,
        )
        copy.start()
        flow["copies"].append(copy)

    for flow in flows:
        start(flow, 0)
    for stage in range(max(len(flow["order"]) for flow in flows)):
        for flow in flows:
            order = flow["order"]
            if stage >= len(order):
                continue
            flow["copies"][stage].wait_recv()
            ref, where = cut(flow, stage, order[stage], mine[order[stage]])
            total = flow["buffers"][stage][...] + ref[where]
            flow["left"].remove(order[stage])
            if stage + 1 < len(order):
                flow["buffers"][stage][...] = total
                start(flow, stage + 1)
            else:
                outs[flow["array"]][flow["rows"]] = total
    for flow in flows:
        for copy in flow["copies"]:
            copy.wait_send()


def per_device(head_emb, tail_emb, relations, head_index, tail_index, rel_index, neg_index):
    heads_n, tails_n = lax.axis_size("head"), lax.axis_size("tail")
    width = relations.shape[1]
    own_rows = relations.shape[0]
    count_rel = own_rows * heads_n * tails_n // width
    heads, tails = head_emb[0], tail_emb[0]
    n_head, n_tail = heads.shape[0], tails.shape[0]
    steps, per_step, batch = head_index.shape[2:]
    negs = neg_index.shape[4]
    blocks = steps * per_step
    vmem = pl.BlockSpec(memory_space=pltpu.VMEM)

    local = [a[0, 0] for a in (head_index, tail_index, rel_index, neg_index)]
    per = [[] for _ in local]
    for s in range(steps):
        shift = s % tails_n
        rows = [a[s] for a in local]
        if shift:
            sent = jnp.concatenate([r.reshape(-1) for r in rows])
            sent = lax.ppermute(sent, "tail", [(i, (i - shift) % tails_n) for i in range(tails_n)])
            cuts, at = [], 0
            for r in rows:
                cuts.append(sent[at:at + r.size].reshape(r.shape))
                at += r.size
            rows = cuts
        for kept, r in zip(per, rows):
            kept.append(r)
    rows_h, rows_t, rows_r, rows_n = [jnp.concatenate(p, axis=0) for p in per]
    if count_rel * n_head * n_tail < 2 ** 31:
        keys = lax.sort((rows_r * n_head + rows_h) * n_tail + rows_t, dimension=1, is_stable=False)
        rows_t = keys % n_tail
        rows_h = (keys // n_tail) % n_head
        rows_r = keys // (n_tail * n_head)
    else:
        rows_r, rows_h, rows_t = lax.sort((rows_r, rows_h, rows_t), dimension=1, num_keys=1)
    bounds = jnp.arange(count_rel + 1, dtype=jnp.int32)
    offsets = jnp.sum((rows_r[:, None, :] < bounds[None, :, None]).astype(jnp.int32), axis=2)

    bits = Bits([("head", heads_n), ("tail", tails_n)])
    count = len(bits.names)
    hb, tb = log2(heads_n), log2(tails_n)
    head_bits, tail_bits = list(range(hb)), list(range(hb, hb + tb))
    core, planar = head_bits[-1:], head_bits[:-1]
    gather_orders = [tail_bits + planar + core, tail_bits + planar[::-1] + core]
    reduce_orders = [core + planar + tail_bits[::-1], core + planar[::-1] + tail_bits[::-1]]

    columns = jnp.stack([rows_h, rows_t, rows_n])[..., None]
    full, hv, tv, nv = pl.pallas_call(
        functools.partial(gather_kernel, bits, gather_orders),
        out_shape=(
            jax.ShapeDtypeStruct((2,) * count + (own_rows, width), F32),
            jax.ShapeDtypeStruct((blocks, batch, width), F32),
            jax.ShapeDtypeStruct((blocks, batch, width), F32),
            jax.ShapeDtypeStruct((blocks, negs, width), F32),
        ),
        in_specs=[vmem] * 4,
        out_specs=(vmem,) * 4,
        scratch_shapes=[
            pltpu.VMEM((n_head, 2 * width), BF16),
            pltpu.VMEM((n_tail, 2 * width), BF16),
            pltpu.SemaphoreType.DMA((2 * count,)),
            pltpu.SemaphoreType.DMA((2 * count,)),
        ],
        compiler_params=pltpu.CompilerParams(
            collective_id=0, has_side_effects=True, vmem_limit_bytes=VMEM_LIMIT
        ),
        name="gather",
    )(relations, heads, tails, columns)

    both = jnp.concatenate([rows_t, rows_n], axis=1).reshape(-1)
    lanes = jnp.stack([jnp.pad(rows_h.reshape(-1), (0, both.shape[0] - blocks * batch)), both])
    head_sum, tail_sum, rel_sum = pl.pallas_call(
        compute_kernel,
        out_shape=(
            jax.ShapeDtypeStruct((n_head, width), F32),
            jax.ShapeDtypeStruct((n_tail, width), F32),
            jax.ShapeDtypeStruct((count_rel * width, width), F32),
        ),
        in_specs=[pl.BlockSpec(memory_space=pltpu.SMEM)] + [vmem] * 5,
        out_specs=(vmem,) * 3,
        scratch_shapes=[
            pltpu.VMEM((count_rel * width, width), BF16),
            pltpu.VMEM((count_rel * width, width), BF16),
            pltpu.VMEM((blocks, batch, width), F32),
            pltpu.VMEM((blocks, batch, width), F32),
            pltpu.VMEM((blocks, batch, width), F32),
            pltpu.VMEM((blocks * (batch + negs), 2 * width), BF16),
        ],
        compiler_params=pltpu.CompilerParams(vmem_limit_bytes=VMEM_LIMIT),
        name="compute",
    )(offsets, full.reshape(count_rel * width, width), hv, tv, nv, lanes)

    plans = [(2, reduce_orders[0], 0, 2), (2, reduce_orders[1], 1, 2)]
    plans += [(1, core + planar, 0, 2), (1, core + planar[::-1], 1, 2)]
    plans += [(0, tail_bits[::-1], 0, 1)]
    inputs = (
        head_sum.reshape((2,) * tb + (n_head // tails_n, width)),
        tail_sum.reshape((2,) * hb + (n_tail // heads_n, width)),
        rel_sum.reshape((2,) * count + (own_rows, width)),
    )
    buffers, sems = [], 0
    for array, order, part, parts in plans:
        rows = inputs[array].shape[-2] // parts
        for stage in range(len(order)):
            buffers.append(pltpu.VMEM((2,) * (len(order) - 1 - stage) + (rows, width), F32))
        sems += len(order)
    head_share, tail_share, rel_share = pl.pallas_call(
        functools.partial(reduce_kernel, bits, plans),
        out_shape=tuple(jax.ShapeDtypeStruct(a.shape[-2:], F32) for a in inputs),
        in_specs=[vmem] * 3,
        out_specs=(vmem,) * 3,
        scratch_shapes=buffers + [pltpu.SemaphoreType.DMA((sems,)), pltpu.SemaphoreType.DMA((sems,))],
        compiler_params=pltpu.CompilerParams(
            collective_id=1, has_side_effects=True, vmem_limit_bytes=VMEM_LIMIT
        ),
        name="reduce",
    )(*inputs)
    return (head_share[None], tail_share[None], rel_share)


def solution(mesh):
    placed = (
        P("head", None, None),
        P("tail", None, None),
        P(("head", "tail"), None),
        P("head", "tail", None, None, None),
        P("head", "tail", None, None, None),
        P("head", "tail", None, None, None),
        P("head", "tail", None, None, None),
    )
    return jax.shard_map(
        per_device,
        mesh=mesh,
        in_specs=placed,
        out_specs=(P("head", "tail", None), P("tail", "head", None), P(("head", "tail"), None)),
        check_vma=False,
    )
```

time: 397 us -> 157 us (0.40); the launches traced: 391 us -> 157 us
  waiting for transfers between devices: 146 us -> 1.37 us
  local copies, waits for them, and re-layouts: 71.4 us -> 13.2 us
  Pallas kernels: 63.6 us -> 121 us
  other arithmetic: 47.3 us -> 2.37 us
  matrix products: 43.1 us -> 0 us
    pallas_call x0 -> x3, Pallas kernels: none -> 121 us  [the longest x1 46.6 us: per_device(): pl.pallas_call(functools.partial(reduce_kernel, bits, plans), out_shape=t...]
    reduce_scatter x4 -> x0, waiting for transfers between devices: 83.3 us -> none  [the longest x1 43.2 us: per_device(): lax.psum_scatter(back_home, 'head', scatter_dimension=0, tiled=True)]
    another operation x4 -> x0, Pallas kernels: 59.6 us -> none
    ppermute x3 -> x1, waiting for transfers between devices: 47.9 us -> 1.37 us  [per_device(): lax.ppermute(sent, 'tail', [(i, (i - shift) % tails_n) for i in range(tai...]
    dot_general x7 -> x0, matrix products: 43.1 us -> none  [the longest x1 31.5 us: per_device(): jnp.einsum('bk,be->ke', spread_all, factor_all, precision=highest)]
    gather x12 -> x0, local copies, waits for them, and re-layouts: 34.9 us -> none  [the longest x2 6.98 us: per_device(): rows_t = tail_index[0, 0, step, 0][order]]
    scatter-add x6 -> x0, other arithmetic: 28.8 us -> none  [the longest x2 10.8 us: per_device(): local.at[rows_n]]
    unnamed x48 -> x6, local copies, waits for them, and re-layouts: 30.2 us -> 4.83 us
  transfers between devices with their start and end apart: 8 -> 1, of which waited for: 6 -> 1; matrix products, arithmetic and copies ran while one was open for 30% -> 0% of each run, Pallas kernels for 9% -> 0%
where the time goes in v1:
time: 157 us
  Pallas kernels  121 us (77%)
  between operations  14.1 us (9%)
  local copies, waits for them, and re-layouts  13.2 us (8%)
  starting transfers between devices  5.13 us (3%)
  other arithmetic  2.37 us (2%)
    pallas_call x1, Pallas kernels, per_device(): pl.pallas_call(functools.partial(reduce_kernel, bits, plans), out_shape=t...  46.6 us
    pallas_call x1, Pallas kernels, per_device(): pl.pallas_call(functools.partial(gather_kernel, bits, gather_orders), out...  41.2 us
    pallas_call x1, Pallas kernels, per_device(): pl.pallas_call(compute_kernel, out_shape=(jax.ShapeDtypeStruct((n_head, w...  33.5 us
    ppermute x1, starting transfers between devices, per_device(): lax.ppermute(sent, 'tail', [(i, (i - shift) % tails_n) for i in range(tai...  5.13 us
    unnamed x6, local copies, waits for them, and re-layouts  4.83 us
    sort x2, local copies, waits for them, and re-layouts, per_device(): lax.sort((rows_r * n_head + rows_h) * n_tail + rows_t, dimension=1, is_st...  3.93 us
  transfers between devices with their start and end apart: 1, of which 1 were waited for; matrix products, arithmetic and copies ran while one was open for 0% of the time, Pallas kernels for 0%

profile of v1, /device:TPU:0, one launch (start us, length us, event | category | flops | bytes accessed | tf_op | source)
XLA Modules:
  0.0 157.5 jit_solution(18365988005369058034)
XLA Ops:
  7.2 0.0 sort.9.cloned.1.call-start
  7.2 0.7 slice_bitcast_fusion.3
  7.9 0.7 slice_bitcast_fusion
  8.6 0.7 slice_bitcast_fusion.1
  9.4 5.1 %collective-permute-start = (s32[2048]{0:T(1024)S(1)}, s32[2048]{0:T(1024)S(1)}, u32[]{:S(2)}, u32[]{:S(2)}) collective-permute-start(s32[2048]{0:T(1024)S(1)} %pad_add_fusion.1), channel_id=1, source_target_pairs={{0,3},{1,0},{2,1},{3,2},{4,7},{5,4},{6,5},{7,6},{8,11},{9,8},{10,9... | collective-permute-start | bytes 24584 | tf_op jit(solution)/shard_map/ppermute | solution.py:312
  14.5 1.4 collective-permute-done
  15.9 0.6 fusion.4
  16.5 0.0 sort.9.cloned.1.call-update
  16.5 3.9 %sort.9.cloned.1.call-done = s32[2,512]{1,0:T(2,128)} async-done(((s32[2,512]{1,0:T(2,128)}), s32[2,512]{1,0:T(2,128)}) %sort.9.cloned.1.call-update) | async-done | bytes 4112 | tf_op jit(solution)/shard_map/sort | solution.py:322
  20.4 0.7 and_select_fusion.1
  21.2 0.4 fusion
  21.5 0.7 copy.12.off_ref
  22.2 1.7 %copy.11.idx_ref = s32[3,2,512,1]{3,2,1,0:T(8,128)} copy(s32[3,2,512,1]{2,1,0,3:T(2,128)S(1)} %add_bitcast_fusion) | data formatting | bytes 24576 | tf_op jit(solution)/shard_map/broadcast_in_dim | solution.py:339
  23.9 0.6 pad_add_fusion.idx_ref
  24.5 41.2 %gather.1 = (f32[2,2,2,2,2,128,256]{6,5,4,3,2,1,0:T(8,128)}, f32[2,512,256]{2,1,0:T(8,128)}, f32[2,512,256]{2,1,0:T(8,128)}, f32[2,512,256]{2,1,0:T(8,128)}) custom-call(f32[128,256]{1,0:T(8,128)} %rel_ref.1, f32[512,256]{1,0:T(8,128)} %bitcast.41, f32[2048,256]{1,0:T(8,128)} %bitcast.39, s32[3,2,512,1]{3,2,1,0:T(8,128)} %copy.11.idx_ref), custom_call_target="tpu_custom_call" | custom-call | tf_op jit(solution)/shard_map/gather/pallas_call | solution.py:340
  65.7 33.5 %compute.1 = (f32[512,256]{1,0:T(8,128)}, f32[2048,256]{1,0:T(8,128)}, f32[4096,256]{1,0:T(8,128)}) custom-call(s32[2,17]{1,0:T(2,128)} %copy.12.off_ref, f32[4096,256]{1,0:T(8,128)} %bitcast.37, f32[2,512,256]{2,1,0:T(8,128)} %get-tuple-element.14.hv_ref, f32[2,512,256]{2,1,0:T(8,128)} %get-tuple-element.15.tv_ref, ...), custom_call_target="tpu_custom_call" | custom-call | tf_op jit(solution)/shard_map/compute/pallas_call | solution.py:364
  99.2 46.6 %reduce.1 = (f32[128,256]{1,0:T(8,128)}, f32[256,256]{1,0:T(8,128)}, f32[128,256]{1,0:T(8,128)}) custom-call(f32[2,2,128,256]{3,2,1,0:T(8,128)} %bitcast.42, f32[2,2,2,256,256]{4,3,2,1,0:T(8,128)} %bitcast.40, f32[2,2,2,2,2,128,256]{6,5,4,3,2,1,0:T(8,128)} %bitcast.38), custom_call_target="tpu_custom_call" | custom-call | tf_op jit(solution)/shard_map/reduce/pallas_call | solution.py:399
  145.8 1.6 copy.18
  147.4 1.7 %copy.19 = f32[1,256,256]{2,1,0:T(8,128)} copy(f32[1,256,256]{2,1,0:T(8,128)} %bitcast.43) | data formatting | bytes 524288
  149.1 1.6 copy.20
  (8 shorter events, 0.1 us)
Async XLA Ops:
  7.2 13.2 %sort.9.cloned.1.call-start = ((), (), s32[]{:S(2)}) async-start(), calls=%async_computation | async-start | bytes 12320 | tf_op jit(solution)/shard_map/sort | solution.py:322
  9.4 6.5 %collective-permute-start = (s32[2048]{0:T(1024)S(1)}, s32[2048]{0:T(1024)S(1)}, u32[]{:S(2)}, u32[]{:S(2)}) collective-permute-start(s32[2048]{0:T(1024)S(1)} %pad_add_fusion.1), channel_id=1, source_target_pairs={{0,3},{1,0},{2,1},{3,2},{4,7},{5,4},{6,5},{7,6},{8,11},{9,8},{10,9... | collective-permute-start | bytes 24584 | tf_op jit(solution)/shard_map/ppermute | solution.py:312
Sparse Core Ops, SparseCore 0:
  16.6 3.5 sort.11.cloned.1.call-done
  (1 shorter events, 0.0 us)

commit v2 on v1

--- a/solution.py
+++ b/solution.py
@@ -9,6 +9,7 @@
 F32 = jnp.float32
 BF16 = jnp.bfloat16
 VMEM_LIMIT = 60 * 1024 * 1024
+GROUPS = 2
 NN = (((1,), (0,)), ((), ()))
 NT = (((1,), (1,)), ((), ()))
 TN = (((0,), (0,)), ((), ()))
@@ -53,16 +54,52 @@
     pl.semaphore_wait(barrier, len(partners))
 
 
+def column(row):
+    return jnp.transpose(jnp.broadcast_to(row, (8, row.shape[1])))[:, :1]
+
+
 def gather_kernel(
-    bits, orders, rel_ref, heads_ref, tails_ref, idx_ref,
-    full_ref, hv_ref, tv_ref, nv_ref, heads_cat, tails_cat, send_sem, recv_sem,
+    bits, orders, tails_n, steps, count_rel, *refs,
 ):
+    rel_ref, heads_ref, tails_ref = refs[:3]
+    sent_idx = refs[3:7]
+    full_ref, hv_ref, tv_ref, nv_ref, off_ref, head_ids, tail_ids = refs[7:14]
+    heads_cat, tails_cat, cols, neg_cols = refs[14:18]
+    got_idx = refs[18:22]
+    send_sem, recv_sem, idx_send, idx_recv = refs[22:]
     count = len(bits.names)
     parts = len(orders)
     rows = rel_ref.shape[0] // parts
     mine = [bits.mine(i) for i in range(count)]
     partner = [bits.partner(i) for i in range(count)]
-    meet(partner)
+    blocks, batch = hv_ref.shape[:2]
+    negs = nv_ref.shape[1]
+    per_step = blocks // steps
+    width = heads_ref.shape[1]
+
+    me = lax.axis_index("tail")
+    around, moves = [], []
+    for s in range(steps):
+        if s % tails_n:
+            to = {"tail": lax.rem(me + tails_n - s % tails_n, tails_n)}
+            around += [to, {"tail": lax.rem(me + s % tails_n, tails_n)}]
+            moves.append((s, to))
+    meet(partner + around)
+    idx_copies = []
+    for s, to in moves:
+        for a in range(4):
+            at = pl.ds(s * per_step, per_step)
+            sem = len(idx_copies)
+            copy = pltpu.make_async_remote_copy(
+                src_ref=sent_idx[a].at[at],
+                dst_ref=got_idx[a].at[at],
+                send_sem=idx_send.at[sem],
+                recv_sem=idx_recv.at[sem],
+                device_id=to,
+                device_id_type=pl.DeviceIdType.MESH,
+            )
+            copy.start()
+            idx_copies.append(copy)
 
     def start(part, stage):
         order = orders[part]
@@ -84,49 +121,87 @@
     copies = [[start(part, 0)] for part in range(parts)]
     full_ref[tuple(mine)] = rel_ref[...]
 
-    blocks, batch = idx_ref.shape[1], idx_ref.shape[2]
-    width = heads_ref.shape[1]
-    tile = 128
-
     def halves(source, cat):
         high, low = split(source[...])
         cat[:, :width] = high
         cat[:, width:] = low
 
-    def take(which, b, cat, out):
+    def arrive():
+        for copy in idx_copies:
+            copy.wait_recv()
+
+    def order_block(b):
+        moved = (b // per_step) % tails_n != 0
+        row = [(got_idx if moved else sent_idx)[a][b] for a in range(4)]
+        rel = column(row[2])
+        lanes = off_ref.shape[2]
+        lane = lax.broadcasted_iota(jnp.int32, (batch, lanes), 1)
+        base = jnp.sum((rel < lane).astype(jnp.int32), axis=0, keepdims=True)
+        off_ref[b] = base
+        same = rel == lane
+        earlier = (
+            lax.broadcasted_iota(jnp.int32, (batch, batch), 1)
+            < lax.broadcasted_iota(jnp.int32, (batch, batch), 0)
+        ).astype(BF16)
+        rank = dot(earlier, same.astype(BF16), NN).astype(jnp.int32)
+        place = jnp.sum(jnp.where(same, rank + base, 0), axis=1, keepdims=True)
+        to = place == lax.broadcasted_iota(jnp.int32, (batch, batch), 1)
+        ids = [jnp.sum(jnp.where(to, column(row[a]), 0), axis=0, keepdims=True) for a in (0, 1)]
+        head_ids[b] = ids[0]
+        tail_ids[:, b * (batch + negs):b * (batch + negs) + batch] = ids[1]
+        tail_ids[:, b * (batch + negs) + batch:(b + 1) * (batch + negs)] = row[3]
+        cols[0, b] = column(ids[0])
+        cols[1, b] = column(ids[1])
+        neg_cols[0, b] = column(row[3])
+
+    def take(source, which, b, cat, out):
+        tile = 128
+
         def body(t, carry):
             at = pl.ds(pl.multiple_of(t * tile, tile), tile)
-            ids = idx_ref[which, b, at]
+            ids = source[which, b, at]
             hot = (ids == lax.broadcasted_iota(jnp.int32, (tile, cat.shape[0]), 1)).astype(BF16)
             both = dot(hot, cat[...], NN)
             out[b, at] = both[:, :width] + both[:, width:]
             return carry
 
-        lax.fori_loop(0, batch // tile, body, 0)
-
-    work = [lambda: (halves(heads_ref, heads_cat), halves(tails_ref, tails_cat))]
-    work += [functools.partial(take, 0, b, heads_cat, hv_ref) for b in range(blocks)]
-    work += [functools.partial(take, 1, b, tails_cat, tv_ref) for b in range(blocks)]
-    work += [functools.partial(take, 2, b, tails_cat, nv_ref) for b in range(blocks)]
-    per = -(-len(work) // count)
-    for stage in range(count):
-        for job in work[stage * per:(stage + 1) * per]:
-            job()
-        for part in range(parts):
-            copies[part][stage].wait_recv()
-            if stage + 1 < count:
-                copies[part].append(start(part, stage + 1))
+        lax.fori_loop(0, out.shape[1] // tile, body, 0)
+
+    work = [lambda: (halves(heads_ref, heads_cat), halves(tails_ref, tails_cat)), arrive]
+    work += [functools.partial(order_block, b) for b in range(blocks)]
+    work += [functools.partial(take, cols, 0, b, heads_cat, hv_ref) for b in range(blocks)]
+    work += [functools.partial(take, cols, 1, b, tails_cat, tv_ref) for b in range(blocks)]
+    work += [functools.partial(take, neg_cols, 0, b, tails_cat, nv_ref) for b in range(blocks)]
+    groups = parts // 2
+    total = count * groups
+    done = 0
+    turn = 0
+    for step in range(count + groups - 1):
+        for group in range(groups):
+            stage = step - group
+            if not 0 <= stage < count:
+                continue
+            turn += 1
+            upto = -(-len(work) * turn // total)
+            for job in work[done:upto]:
+                job()
+            done = upto
+            for part in (2 * group, 2 * group + 1):
+                copies[part][stage].wait_recv()
+                if stage + 1 < count:
+                    copies[part].append(start(part, stage + 1))
+    for copy in idx_copies:
+        copy.wait_send()
     for part in range(parts):
         for copy in copies[part]:
             copy.wait_send()
 
 
 def compute_kernel(
-    off_ref, rel_ref, hv_ref, tv_ref, nv_ref, idx_ref,
-    head_ref, tail_ref, grad_ref,
-    rel_hi, rel_lo, query, factor, through, spread,
+    relations, off_ref, rel_ref, hv_ref, tv_ref, nv_ref,
+    back_ref, spread, grad_ref,
+    rel_hi, rel_lo, query, factor, through,
 ):
-    relations = off_ref.shape[1] - 1
     blocks, batch, width = hv_ref.shape
     negs = nv_ref.shape[1]
     window = 64
@@ -143,8 +218,8 @@
 
     def over_windows(step, after=None):
         def one(r, carry):
-            low = [off_ref[b, r] for b in range(blocks)]
-            high = [off_ref[b, r + 1] for b in range(blocks)]
+            low = [off_ref[b, 0, r] for b in range(blocks)]
+            high = [off_ref[b, 0, r + 1] for b in range(blocks)]
             base = [low[b] // 8 * 8 for b in range(blocks)]
             trips = jnp.int32(0)
             for b in range(blocks):
@@ -210,38 +285,29 @@
     over_windows(outer)
     over_windows(apply(factor, through, NT))
 
-    tile = 256
-    ids = idx_ref[1:2, :]
-
-    def scatter(t, carry):
-        at = pl.ds(pl.multiple_of(t * tile, tile), tile)
-        hot = (ids == lax.broadcasted_iota(jnp.int32, (tile, ids.shape[1]), 0) + t * tile).astype(BF16)
-        both = dot(hot, spread[...], NN)
-        tail_ref[at] = both[:, :width] + both[:, width:]
-        return carry
-
-    lax.fori_loop(0, tail_ref.shape[0] // tile, scatter, 0)
-    hids = idx_ref[0:1, :blocks * batch]
-    hot = (hids == lax.broadcasted_iota(jnp.int32, (head_ref.shape[0], hids.shape[1]), 0)).astype(BF16)
-    high, low = split(through[...].reshape(blocks * batch, width))
-    head_ref[...] = dot(hot, high, NN) + dot(hot, low, NN)
-
-
-def reduce_kernel(bits, plans, *refs):
-    inputs = refs[:3]
-    outs = refs[3:6]
-    buffers = refs[6:-2]
+    for b in range(blocks):
+        high, low = split(through[b])
+        back_ref[pl.ds(b * batch, batch), :width] = high
+        back_ref[pl.ds(b * batch, batch), width:] = low
+
+
+def reduce_kernel(bits, plans, grad_ref, spread, back, tail_ids, head_ids, *refs):
+    outs = refs[:3]
+    head_sum, tail_sum = refs[3:5]
+    buffers = refs[5:-2]
     send_sem, recv_sem = refs[-2:]
+    inputs = (head_sum, tail_sum, grad_ref)
+    width = grad_ref.shape[-1]
     mine = [bits.mine(i) for i in range(len(bits.names))]
     partner = [bits.partner(i) for i in range(len(bits.names))]
     meet(partner)
     flows = []
     sem = 0
     buf = 0
-    for array, order, part, parts in plans:
+    for array, order, part, parts, group in plans:
         rows = inputs[array].shape[-2] // parts
         flows.append(dict(
-            array=array, order=order, rows=pl.ds(part * rows, rows), sem=sem,
+            array=array, order=order, rows=pl.ds(part * rows, rows), sem=sem, group=group,
             buffers=buffers[buf:buf + len(order)], left=sorted(order), copies=[],
         ))
         sem += len(order)
@@ -269,12 +335,36 @@
         copy.start()
         flow["copies"].append(copy)
 
-    for flow in flows:
-        start(flow, 0)
-    for stage in range(max(len(flow["order"]) for flow in flows)):
+    def begin(array):
+        for flow in flows:
+            if flow["array"] == array:
+                start(flow, 0)
+
+    def scatter(ids, source, out):
+        dims = len(out.shape) - 2
+        rows = out.shape[-2]
+
+        def body(t, carry):
+            hot = (ids == lax.broadcasted_iota(jnp.int32, (rows, ids.shape[1]), 0) + t * rows)
+            both = dot(hot.astype(BF16), source[...], NN)
+            where = tuple(lax.rem(t // (1 << i), 2) for i in reversed(range(dims)))
+            out[where] = both[:, :width] + both[:, width:]
+            return carry
+
+        lax.fori_loop(0, 1 << dims, body, 0)
+
+    begin(2)
+    heads = jnp.concatenate([head_ids[b] for b in range(head_ids.shape[0])], axis=1)
+    scatter(heads, back, head_sum)
+    begin(0)
+    scatter(tail_ids[...], spread, tail_sum)
+    begin(1)
+    groups = 1 + max(flow["group"] for flow in flows)
+    for step in range(len(bits.names) + groups - 1):
         for flow in flows:
             order = flow["order"]
-            if stage >= len(order):
+            stage = step - flow["group"]
+            if not 0 <= stage < len(order):
                 continue
             flow["copies"][stage].wait_recv()
             ref, where = cut(flow, stage, order[stage], mine[order[stage]])
@@ -290,6 +380,11 @@
             copy.wait_send()
 
 
+def finish_kernel(*refs):
+    for source, out in zip(refs[:3], refs[3:]):
+        out[...] = source[...]
+
+
 def per_device(head_emb, tail_emb, relations, head_index, tail_index, rel_index, neg_index):
     heads_n, tails_n = lax.axis_size("head"), lax.axis_size("tail")
     width = relations.shape[1]
@@ -300,75 +395,61 @@
     steps, per_step, batch = head_index.shape[2:]
     negs = neg_index.shape[4]
     blocks = steps * per_step
+    each = batch + negs
+    lanes = (count_rel + 128) // 128 * 128
     vmem = pl.BlockSpec(memory_space=pltpu.VMEM)
-
-    local = [a[0, 0] for a in (head_index, tail_index, rel_index, neg_index)]
-    per = [[] for _ in local]
-    for s in range(steps):
-        shift = s % tails_n
-        rows = [a[s] for a in local]
-        if shift:
-            sent = jnp.concatenate([r.reshape(-1) for r in rows])
-            sent = lax.ppermute(sent, "tail", [(i, (i - shift) % tails_n) for i in range(tails_n)])
-            cuts, at = [], 0
-            for r in rows:
-                cuts.append(sent[at:at + r.size].reshape(r.shape))
-                at += r.size
-            rows = cuts
-        for kept, r in zip(per, rows):
-            kept.append(r)
-    rows_h, rows_t, rows_r, rows_n = [jnp.concatenate(p, axis=0) for p in per]
-    if count_rel * n_head * n_tail < 2 ** 31:
-        keys = lax.sort((rows_r * n_head + rows_h) * n_tail + rows_t, dimension=1, is_stable=False)
-        rows_t = keys % n_tail
-        rows_h = (keys // n_tail) % n_head
-        rows_r = keys // (n_tail * n_head)
-    else:
-        rows_r, rows_h, rows_t = lax.sort((rows_r, rows_h, rows_t), dimension=1, num_keys=1)
-    bounds = jnp.arange(count_rel + 1, dtype=jnp.int32)
-    offsets = jnp.sum((rows_r[:, None, :] < bounds[None, :, None]).astype(jnp.int32), axis=2)
+    shape = jax.ShapeDtypeStruct
 
     bits = Bits([("head", heads_n), ("tail", tails_n)])
     count = len(bits.names)
     hb, tb = log2(heads_n), log2(tails_n)
     head_bits, tail_bits = list(range(hb)), list(range(hb, hb + tb))
     core, planar = head_bits[-1:], head_bits[:-1]
-    gather_orders = [tail_bits + planar + core, tail_bits + planar[::-1] + core]
+    groups = min(GROUPS, own_rows // 16)
+    gather_orders = [tail_bits + planar + core, tail_bits + planar[::-1] + core] * groups
     reduce_orders = [core + planar + tail_bits[::-1], core + planar[::-1] + tail_bits[::-1]]
 
-    columns = jnp.stack([rows_h, rows_t, rows_n])[..., None]
-    full, hv, tv, nv = pl.pallas_call(
-        functools.partial(gather_kernel, bits, gather_orders),
+    indices = [
+        a.reshape(blocks, 1, a.shape[-1]) for a in (head_index, tail_index, rel_index, neg_index)
+    ]
+    full, hv, tv, nv, offsets, head_ids, tail_ids = pl.pallas_call(
+        functools.partial(gather_kernel, bits, gather_orders, tails_n, steps, count_rel),
         out_shape=(
-            jax.ShapeDtypeStruct((2,) * count + (own_rows, width), F32),
-            jax.ShapeDtypeStruct((blocks, batch, width), F32),
-            jax.ShapeDtypeStruct((blocks, batch, width), F32),
-            jax.ShapeDtypeStruct((blocks, negs, width), F32),
+            shape((2,) * count + (own_rows, width), F32),
+            shape((blocks, batch, width), F32),
+            shape((blocks, batch, width), F32),
+            shape((blocks, negs, width), F32),
+            shape((blocks, 1, lanes), jnp.int32),
+            shape((blocks, 1, batch), jnp.int32),
+            shape((1, blocks * each), jnp.int32),
         ),
-        in_specs=[vmem] * 4,
-        out_specs=(vmem,) * 4,
+        in_specs=[vmem] * 7,
+        out_specs=(vmem,) * 7,
         scratch_shapes=[
             pltpu.VMEM((n_head, 2 * width), BF16),
             pltpu.VMEM((n_tail, 2 * width), BF16),
-            pltpu.SemaphoreType.DMA((2 * count,)),
-            pltpu.SemaphoreType.DMA((2 * count,)),
+            pltpu.VMEM((2, blocks, batch, 1), jnp.int32),
+            pltpu.VMEM((1, blocks, negs, 1), jnp.int32),
+        ] + [pltpu.VMEM(a.shape, jnp.int32) for a in indices] + [
+            pltpu.SemaphoreType.DMA((len(gather_orders) * count,)),
+            pltpu.SemaphoreType.DMA((len(gather_orders) * count,)),
+            pltpu.SemaphoreType.DMA((4 * steps,)),
+            pltpu.SemaphoreType.DMA((4 * steps,)),
         ],
         compiler_params=pltpu.CompilerParams(
             collective_id=0, has_side_effects=True, vmem_limit_bytes=VMEM_LIMIT
         ),
         name="gather",
-    )(relations, heads, tails, columns)
-
-    both = jnp.concatenate([rows_t, rows_n], axis=1).reshape(-1)
-    lanes = jnp.stack([jnp.pad(rows_h.reshape(-1), (0, both.shape[0] - blocks * batch)), both])
-    head_sum, tail_sum, rel_sum = pl.pallas_call(
-        compute_kernel,
+    )(relations, heads, tails, *indices)
+
+    back, spread, rel_sum = pl.pallas_call(
+        functools.partial(compute_kernel, count_rel),
         out_shape=(
-            jax.ShapeDtypeStruct((n_head, width), F32),
-            jax.ShapeDtypeStruct((n_tail, width), F32),
-            jax.ShapeDtypeStruct((count_rel * width, width), F32),
+            shape((blocks * batch, 2 * width), BF16),
+            shape((blocks * each, 2 * width), BF16),
+            shape((count_rel * width, width), F32),
         ),
-        in_specs=[pl.BlockSpec(memory_space=pltpu.SMEM)] + [vmem] * 5,
+        in_specs=[pl.BlockSpec(memory_space=pltpu.SMEM)] + [vmem] * 4,
         out_specs=(vmem,) * 3,
         scratch_shapes=[
             pltpu.VMEM((count_rel * width, width), BF16),
@@ -376,37 +457,50 @@
             pltpu.VMEM((blocks, batch, width), F32),
             pltpu.VMEM((blocks, batch, width), F32),
             pltpu.VMEM((blocks, batch, width), F32),
-            pltpu.VMEM((blocks * (batch + negs), 2 * width), BF16),
         ],
         compiler_params=pltpu.CompilerParams(vmem_limit_bytes=VMEM_LIMIT),
         name="compute",
-    )(offsets, full.reshape(count_rel * width, width), hv, tv, nv, lanes)
-
-    plans = [(2, reduce_orders[0], 0, 2), (2, reduce_orders[1], 1, 2)]
-    plans += [(1, core + planar, 0, 2), (1, core + planar[::-1], 1, 2)]
-    plans += [(0, tail_bits[::-1], 0, 1)]
-    inputs = (
-        head_sum.reshape((2,) * tb + (n_head // tails_n, width)),
-        tail_sum.reshape((2,) * hb + (n_tail // heads_n, width)),
-        rel_sum.reshape((2,) * count + (own_rows, width)),
+    )(offsets, full.reshape(count_rel * width, width), hv, tv, nv)
+
+    sizes = (
+        (2,) * tb + (n_head // tails_n, width),
+        (2,) * hb + (n_tail // heads_n, width),
+        (2,) * count + (own_rows, width),
     )
+    plans = []
+    for group in range(groups):
+        plans += [(2, reduce_orders[i], 2 * group + i, 2 * groups, group) for i in range(2)]
+        plans += [
+            (1, (core + planar, core + planar[::-1])[i], 2 * group + i, 2 * groups, group)
+            for i in range(2)
+        ]
+    plans += [(0, tail_bits[::-1], 0, 1, 0)]
     buffers, sems = [], 0
-    for array, order, part, parts in plans:
-        rows = inputs[array].shape[-2] // parts
+    for array, order, part, parts, group in plans:
+        rows = sizes[array][-2] // parts
         for stage in range(len(order)):
             buffers.append(pltpu.VMEM((2,) * (len(order) - 1 - stage) + (rows, width), F32))
         sems += len(order)
-    head_share, tail_share, rel_share = pl.pallas_call(
+    shares = tuple(shape(a[-2:], F32) for a in sizes)
+    totals = pl.pallas_call(
         functools.partial(reduce_kernel, bits, plans),
-        out_shape=tuple(jax.ShapeDtypeStruct(a.shape[-2:], F32) for a in inputs),
-        in_specs=[vmem] * 3,
+        out_shape=shares,
+        in_specs=[vmem] * 5,
         out_specs=(vmem,) * 3,
-        scratch_shapes=buffers + [pltpu.SemaphoreType.DMA((sems,)), pltpu.SemaphoreType.DMA((sems,))],
+        scratch_shapes=[pltpu.VMEM(sizes[0], F32), pltpu.VMEM(sizes[1], F32)] + buffers
+        + [pltpu.SemaphoreType.DMA((sems,)), pltpu.SemaphoreType.DMA((sems,))],
         compiler_params=pltpu.CompilerParams(
             collective_id=1, has_side_effects=True, vmem_limit_bytes=VMEM_LIMIT
         ),
         name="reduce",
-    )(*inputs)
+    )(rel_sum.reshape(sizes[2]), spread, back, tail_ids, head_ids)
+    head_share, tail_share, rel_share = pl.pallas_call(
+        finish_kernel,
+        out_shape=shares,
+        in_specs=[vmem] * 3,
+        out_specs=(vmem,) * 3,
+        name="finish",
+    )(*totals)
     return (head_share[None], tail_share[None], rel_share)
 
 

time: 157 us -> 122 us (0.78)
  between operations: 14.1 us -> 0.65 us
  local copies, waits for them, and re-layouts: 13.2 us -> 0 us
  starting transfers between devices: 5.13 us -> 0 us
  other arithmetic: 2.37 us -> 0 us
    ppermute x1 -> x0, starting transfers between devices: 5.13 us -> none  [per_device(): lax.ppermute(sent, 'tail', [(i, (i - shift) % tails_n) for i in range(tai...]
    unnamed x6 -> x0, local copies, waits for them, and re-layouts: 4.83 us -> none
    sort x2 -> x0, local copies, waits for them, and re-layouts: 3.93 us -> none  [per_device(): lax.sort((rows_r * n_head + rows_h) * n_tail + rows_t, dimension=1, is_st...]
    squeeze x3 -> x0, local copies, waits for them, and re-layouts: 2.13 us -> none  [per_device(): rows = [a[s] for a in local]]
    broadcast_in_dim x1 -> x0, local copies, waits for them, and re-layouts: 1.67 us -> none  [per_device(): columns = jnp.stack([rows_h, rows_t, rows_n])[..., None]]
    pallas_call x3 -> x4, Pallas kernels: 121 us -> 121 us  [the longest x1 51.5 us: per_device(): pl.pallas_call(functools.partial(reduce_kernel, bits, plans), out_shape=s...]
  transfers between devices with their start and end apart: 1 -> 0, of which waited for: 1 -> 0; matrix products, arithmetic and copies ran while one was open for 0% -> 0% of each run, Pallas kernels for 0% -> 0%
where the time goes in v2:
time: 122 us
  Pallas kernels  121 us (99%)
    pallas_call x1, Pallas kernels, per_device(): pl.pallas_call(functools.partial(reduce_kernel, bits, plans), out_shape=s...  51.5 us
    pallas_call x1, Pallas kernels, per_device(): pl.pallas_call(functools.partial(gather_kernel, bits, gather_orders, tail...  40.6 us
    pallas_call x1, Pallas kernels, per_device(): pl.pallas_call(functools.partial(compute_kernel, count_rel), out_shape=(s...  27.3 us

profile of v2, /device:TPU:0, one launch (start us, length us, event | category | flops | bytes accessed | tf_op | source)
XLA Modules:
  0.0 121.9 jit_solution(9548151463840390675)
XLA Ops:
  0.6 40.6 %gather.1 = (f32[2,2,2,2,2,128,256]{6,5,4,3,2,1,0:T(8,128)}, f32[2,512,256]{2,1,0:T(8,128)}, f32[2,512,256]{2,1,0:T(8,128)}, f32[2,512,256]{2,1,0:T(8,128)}, s32...) custom-call(f32[128,256]{1,0:T(8,128)} %refs_0_.1, f32[512,256]{1,0:T(8,128)} %bitcast.13, ...), custom_call_target="tpu_custom_call" | custom-call | tf_op jit(solution)/shard_map/gather/pallas_call | solution.py:415
  41.3 27.3 %compute.1 = (bf16[1024,512]{1,0:T(8,128)(2,1)}, bf16[2048,512]{1,0:T(8,128)(2,1)}, f32[4096,256]{1,0:T(8,128)}) custom-call(s32[2,1,128]{2,1,0:T(1,128)} %get-tuple-element.19.off_ref, f32[4096,256]{1,0:T(8,128)} %bitcast.11, f32[2,512,256]{2,1,0:T(8,128)} %get-tuple-element.21.hv_ref, f32[2,512,256]{2,1,0:T(8,128)} %get-tuple-element.22.tv_ref, ...), custom_call_target="tpu_custom_call" | custom-call | tf_op jit(solution)/shard_map/compute/pallas_call | solution.py:445
  68.6 51.5 %reduce.1 = (f32[128,256]{1,0:T(8,128)}, f32[256,256]{1,0:T(8,128)}, f32[128,256]{1,0:T(8,128)}) custom-call(f32[2,2,2,2,2,128,256]{6,5,4,3,2,1,0:T(8,128)} %bitcast.10, bf16[2048,512]{1,0:T(8,128)(2,1)} %get-tuple-element.25.spread, bf16[1024,512]{1,0:T(8,128)(2,1)} %get-tuple-element.26.back, s32[1,2048]{1,0:T(1,128)} %get-tuple-element.27.tail_ids, ...), custom_call_target="tpu_custom_call" | custom-call | tf_op jit(solution)/shard_map/reduce/pallas_call | solution.py:485
  120.1 1.9 %finish.1 = (f32[128,256]{1,0:T(8,128)}, f32[256,256]{1,0:T(8,128)}, f32[128,256]{1,0:T(8,128)}) custom-call(f32[128,256]{1,0:T(8,128)} %get-tuple-element.29.refs_0_, f32[256,256]{1,0:T(8,128)} %get-tuple-element.30.refs_1_, f32[128,256]{1,0:T(8,128)} %get-tuple-element.31.refs_2_), custom_call_target="tpu_custom_call" | custom-call | tf_op jit(solution)/shard_map/finish/pallas_call | solution.py:497

commit v3 on v2

--- a/solution.py
+++ b/solution.py
@@ -9,7 +9,8 @@
 F32 = jnp.float32
 BF16 = jnp.bfloat16
 VMEM_LIMIT = 60 * 1024 * 1024
-GROUPS = 2
+GATHER_EARLY = 0.375
+REDUCE_EARLY = 0.375
 NN = (((1,), (0,)), ((), ()))
 NT = (((1,), (1,)), ((), ()))
 TN = (((0,), (0,)), ((), ()))
@@ -45,6 +46,16 @@
         axis, bit = self.names[i]
         here = lax.axis_index(axis)
         return {axis: here + (1 << bit) * (1 - 2 * self.mine(i))}
+
+
+def share(rows, early, orders):
+    small = max(8, int(rows * early / 16) * 8)
+    big = rows // 2 - small
+    cuts, first = [], 0
+    for order, size in zip(orders, (big, big, small, small)):
+        cuts.append((order, first, size))
+        first += size
+    return cuts
 
 
 def meet(partners):
@@ -69,7 +80,6 @@
     send_sem, recv_sem, idx_send, idx_recv = refs[22:]
     count = len(bits.names)
     parts = len(orders)
-    rows = rel_ref.shape[0] // parts
     mine = [bits.mine(i) for i in range(count)]
     partner = [bits.partner(i) for i in range(count)]
     blocks, batch = hv_ref.shape[:2]
@@ -102,11 +112,11 @@
             idx_copies.append(copy)
 
     def start(part, stage):
-        order = orders[part]
+        order, first, rows = orders[part]
         done = set(order[:stage])
         where = tuple(slice(None) if i in done else mine[i] for i in range(count))
-        where = where + (pl.ds(part * rows, rows),)
-        source = rel_ref.at[pl.ds(part * rows, rows)] if stage == 0 else full_ref.at[where]
+        where = where + (pl.ds(first, rows),)
+        source = rel_ref.at[pl.ds(first, rows)] if stage == 0 else full_ref.at[where]
         copy = pltpu.make_async_remote_copy(
             src_ref=source,
             dst_ref=full_ref.at[where],
@@ -172,24 +182,16 @@
     work += [functools.partial(take, cols, 0, b, heads_cat, hv_ref) for b in range(blocks)]
     work += [functools.partial(take, cols, 1, b, tails_cat, tv_ref) for b in range(blocks)]
     work += [functools.partial(take, neg_cols, 0, b, tails_cat, nv_ref) for b in range(blocks)]
-    groups = parts // 2
-    total = count * groups
     done = 0
-    turn = 0
-    for step in range(count + groups - 1):
-        for group in range(groups):
-            stage = step - group
-            if not 0 <= stage < count:
-                continue
-            turn += 1
-            upto = -(-len(work) * turn // total)
-            for job in work[done:upto]:
-                job()
-            done = upto
-            for part in (2 * group, 2 * group + 1):
-                copies[part][stage].wait_recv()
-                if stage + 1 < count:
-                    copies[part].append(start(part, stage + 1))
+    for stage in range(count):
+        upto = -(-len(work) * (stage + 1) // count)
+        for job in work[done:upto]:
+            job()
+        done = upto
+        for part in range(parts):
+            copies[part][stage].wait_recv()
+            if stage + 1 < count:
+                copies[part].append(start(part, stage + 1))
     for copy in idx_copies:
         copy.wait_send()
     for part in range(parts):
@@ -304,10 +306,9 @@
     flows = []
     sem = 0
     buf = 0
-    for array, order, part, parts, group in plans:
-        rows = inputs[array].shape[-2] // parts
+    for array, order, first, rows in plans:
         flows.append(dict(
-            array=array, order=order, rows=pl.ds(part * rows, rows), sem=sem, group=group,
+            array=array, order=order, rows=pl.ds(first, rows), sem=sem,
             buffers=buffers[buf:buf + len(order)], left=sorted(order), copies=[],
         ))
         sem += len(order)
@@ -359,12 +360,10 @@
     begin(0)
     scatter(tail_ids[...], spread, tail_sum)
     begin(1)
-    groups = 1 + max(flow["group"] for flow in flows)
-    for step in range(len(bits.names) + groups - 1):
+    for stage in range(len(bits.names)):
         for flow in flows:
             order = flow["order"]
-            stage = step - flow["group"]
-            if not 0 <= stage < len(order):
+            if stage >= len(order):
                 continue
             flow["copies"][stage].wait_recv()
             ref, where = cut(flow, stage, order[stage], mine[order[stage]])
@@ -405,9 +404,15 @@
     hb, tb = log2(heads_n), log2(tails_n)
     head_bits, tail_bits = list(range(hb)), list(range(hb, hb + tb))
     core, planar = head_bits[-1:], head_bits[:-1]
-    groups = min(GROUPS, own_rows // 16)
-    gather_orders = [tail_bits + planar + core, tail_bits + planar[::-1] + core] * groups
-    reduce_orders = [core + planar + tail_bits[::-1], core + planar[::-1] + tail_bits[::-1]]
+    back_planar = planar[::-1]
+    gather_orders = share(own_rows, GATHER_EARLY, [
+        tail_bits + planar + core, tail_bits + back_planar + core,
+        planar + tail_bits + core, back_planar + tail_bits + core,
+    ])
+    reduce_orders = share(own_rows, REDUCE_EARLY, [
+        core + planar + tail_bits[::-1], core + back_planar + tail_bits[::-1],
+        core + tail_bits[::-1] + planar, core + tail_bits[::-1] + back_planar,
+    ])
 
     indices = [
         a.reshape(blocks, 1, a.shape[-1]) for a in (head_index, tail_index, rel_index, neg_index)
@@ -467,17 +472,12 @@
         (2,) * hb + (n_tail // heads_n, width),
         (2,) * count + (own_rows, width),
     )
-    plans = []
-    for group in range(groups):
-        plans += [(2, reduce_orders[i], 2 * group + i, 2 * groups, group) for i in range(2)]
-        plans += [
-            (1, (core + planar, core + planar[::-1])[i], 2 * group + i, 2 * groups, group)
-            for i in range(2)
-        ]
-    plans += [(0, tail_bits[::-1], 0, 1, 0)]
+    plans = [(2, *cut) for cut in reduce_orders]
+    half = sizes[1][-2] // 2
+    plans += [(1, core + planar, 0, half), (1, core + back_planar, half, half)]
+    plans += [(0, tail_bits[::-1], 0, sizes[0][-2])]
     buffers, sems = [], 0
-    for array, order, part, parts, group in plans:
-        rows = sizes[array][-2] // parts
+    for array, order, first, rows in plans:
         for stage in range(len(order)):
             buffers.append(pltpu.VMEM((2,) * (len(order) - 1 - stage) + (rows, width), F32))
         sems += len(order)

time: 122 us -> 109 us (0.89); the launches traced: 122 us -> 107 us
  Pallas kernels: 121 us -> 107 us
    pallas_call x1, Pallas kernels: 51.5 us -> 40.4 us  [per_device(): pl.pallas_call(functools.partial(reduce_kernel, bits, plans), out_shape=s...]
    pallas_call x1, Pallas kernels: 40.6 us -> 37.1 us  [per_device(): pl.pallas_call(functools.partial(gather_kernel, bits, gather_orders, tail...]
where the time goes in v3:
time: 109 us; the launch traced here: 107 us
  Pallas kernels  107 us (98%)
    pallas_call x1, Pallas kernels, per_device(): pl.pallas_call(functools.partial(reduce_kernel, bits, plans), out_shape=s...  40.4 us
    pallas_call x1, Pallas kernels, per_device(): pl.pallas_call(functools.partial(gather_kernel, bits, gather_orders, tail...  37.1 us
    pallas_call x1, Pallas kernels, per_device(): pl.pallas_call(functools.partial(compute_kernel, count_rel), out_shape=(s...  27.3 us

profile of v3, /device:TPU:0, one launch (start us, length us, event | category | flops | bytes accessed | tf_op | source)
XLA Modules:
  0.0 107.3 jit_solution(14210067117732821707)
XLA Ops:
  0.6 37.1 %gather.1 = (f32[2,2,2,2,2,128,256]{6,5,4,3,2,1,0:T(8,128)}, f32[2,512,256]{2,1,0:T(8,128)}, f32[2,512,256]{2,1,0:T(8,128)}, f32[2,512,256]{2,1,0:T(8,128)}, s32...) custom-call(f32[128,256]{1,0:T(8,128)} %refs_0_.1, f32[512,256]{1,0:T(8,128)} %bitcast.13, ...), custom_call_target="tpu_custom_call" | custom-call | tf_op jit(solution)/shard_map/gather/pallas_call | solution.py:420
  37.7 27.3 %compute.1 = (bf16[1024,512]{1,0:T(8,128)(2,1)}, bf16[2048,512]{1,0:T(8,128)(2,1)}, f32[4096,256]{1,0:T(8,128)}) custom-call(s32[2,1,128]{2,1,0:T(1,128)} %get-tuple-element.19.off_ref, f32[4096,256]{1,0:T(8,128)} %bitcast.11, f32[2,512,256]{2,1,0:T(8,128)} %get-tuple-element.21.hv_ref, f32[2,512,256]{2,1,0:T(8,128)} %get-tuple-element.22.tv_ref, ...), custom_call_target="tpu_custom_call" | custom-call | tf_op jit(solution)/shard_map/compute/pallas_call | solution.py:450
  65.0 40.4 %reduce.1 = (f32[128,256]{1,0:T(8,128)}, f32[256,256]{1,0:T(8,128)}, f32[128,256]{1,0:T(8,128)}) custom-call(f32[2,2,2,2,2,128,256]{6,5,4,3,2,1,0:T(8,128)} %bitcast.10, bf16[2048,512]{1,0:T(8,128)(2,1)} %get-tuple-element.25.spread, bf16[1024,512]{1,0:T(8,128)(2,1)} %get-tuple-element.26.back, s32[1,2048]{1,0:T(1,128)} %get-tuple-element.27.tail_ids, ...), custom_call_target="tpu_custom_call" | custom-call | tf_op jit(solution)/shard_map/reduce/pallas_call | solution.py:485
  105.4 1.9 %finish.1 = (f32[128,256]{1,0:T(8,128)}, f32[256,256]{1,0:T(8,128)}, f32[128,256]{1,0:T(8,128)}) custom-call(f32[128,256]{1,0:T(8,128)} %get-tuple-element.29.refs_0_, f32[256,256]{1,0:T(8,128)} %get-tuple-element.30.refs_1_, f32[128,256]{1,0:T(8,128)} %get-tuple-element.31.refs_2_), custom_call_target="tpu_custom_call" | custom-call | tf_op jit(solution)/shard_map/finish/pallas_call | solution.py:497

commit v4 on v3

--- a/solution.py
+++ b/solution.py
@@ -284,8 +284,13 @@
         f = split(jnp.concatenate([factor[b, places[b]] for b in range(blocks)], axis=0))
         grad_ref[at_r] += dot3(x, f, TN)
 
-    over_windows(outer)
-    over_windows(apply(factor, through, NT))
+    back = apply(factor, through, NT)
+
+    def both_ways(at_r, places, masks):
+        outer(at_r, places, masks)
+        back(at_r, places, masks)
+
+    over_windows(both_ways)
 
     for b in range(blocks):
         high, low = split(through[b])

time: 109 us -> 105 us (0.963)
  the two profiles are of different devices: /device:TPU:0 before, /device:TPU:8 now
where the time goes in v4:
time: 105 us
  Pallas kernels  105 us (100%)
    pallas_call x1, Pallas kernels, per_device(): pl.pallas_call(functools.partial(reduce_kernel, bits, plans), out_shape=s...  45.3 us
    pallas_call x1, Pallas kernels, per_device(): pl.pallas_call(functools.partial(gather_kernel, bits, gather_orders, tail...  34.2 us
    pallas_call x1, Pallas kernels, per_device(): pl.pallas_call(functools.partial(compute_kernel, count_rel), out_shape=(s...  23.2 us

profile of v4, /device:TPU:8, one launch (start us, length us, event | category | flops | bytes accessed | tf_op | source)
XLA Modules:
  0.0 105.2 jit_solution(11841379788389485057)
XLA Ops:
  0.6 34.2 %gather.1 = (f32[2,2,2,2,2,128,256]{6,5,4,3,2,1,0:T(8,128)}, f32[2,512,256]{2,1,0:T(8,128)}, f32[2,512,256]{2,1,0:T(8,128)}, f32[2,512,256]{2,1,0:T(8,128)}, s32...) custom-call(f32[128,256]{1,0:T(8,128)} %refs_0_.1, f32[512,256]{1,0:T(8,128)} %bitcast.13, ...), custom_call_target="tpu_custom_call" | custom-call | tf_op jit(solution)/shard_map/gather/pallas_call | solution.py:425
  34.8 23.2 %compute.1 = (bf16[1024,512]{1,0:T(8,128)(2,1)}, bf16[2048,512]{1,0:T(8,128)(2,1)}, f32[4096,256]{1,0:T(8,128)}) custom-call(s32[2,1,128]{2,1,0:T(1,128)} %get-tuple-element.19.off_ref, f32[4096,256]{1,0:T(8,128)} %bitcast.11, f32[2,512,256]{2,1,0:T(8,128)} %get-tuple-element.21.hv_ref, f32[2,512,256]{2,1,0:T(8,128)} %get-tuple-element.22.tv_ref, ...), custom_call_target="tpu_custom_call" | custom-call | tf_op jit(solution)/shard_map/compute/pallas_call | solution.py:455
  58.1 45.3 %reduce.1 = (f32[128,256]{1,0:T(8,128)}, f32[256,256]{1,0:T(8,128)}, f32[128,256]{1,0:T(8,128)}) custom-call(f32[2,2,2,2,2,128,256]{6,5,4,3,2,1,0:T(8,128)} %bitcast.10, bf16[2048,512]{1,0:T(8,128)(2,1)} %get-tuple-element.25.spread, bf16[1024,512]{1,0:T(8,128)(2,1)} %get-tuple-element.26.back, s32[1,2048]{1,0:T(1,128)} %get-tuple-element.27.tail_ids, ...), custom_call_target="tpu_custom_call" | custom-call | tf_op jit(solution)/shard_map/reduce/pallas_call | solution.py:490
  103.3 1.9 %finish.1 = (f32[128,256]{1,0:T(8,128)}, f32[256,256]{1,0:T(8,128)}, f32[128,256]{1,0:T(8,128)}) custom-call(f32[128,256]{1,0:T(8,128)} %get-tuple-element.29.refs_0_, f32[256,256]{1,0:T(8,128)} %get-tuple-element.30.refs_1_, f32[128,256]{1,0:T(8,128)} %get-tuple-element.31.refs_2_), custom_call_target="tpu_custom_call" | custom-call | tf_op jit(solution)/shard_map/finish/pallas_call | solution.py:502
